TPU v7x, 32 devices: a whole 2x2x4 slice. The times are simulated.
32 devices in a mesh: rep: 4 (over y, x), fsdp: 8 (over z, core).
Axes of the slice: x: 2, y: 2, z: 4, core: 2. Of those that a mesh axis runs over, the one named last changes fastest.
Arguments:
- tokens: float32 [4096, 1024], P(('rep', 'fsdp')), may hold values from -6 to 6
- segment_ids: int32 [4096], replicated, may hold values from 0 to 7, never falling along the last dimension, each value on 1 to 1024 neighbouring positions
- cotangent: float32 [4096, 1024], P(('rep', 'fsdp')), may hold values from -6 to 6
- w_qkv: bfloat16 [1024, 2048], P('fsdp'), may hold values from -0.1875 to 0.1875
- w_out: bfloat16 [1024, 1024], P('fsdp'), may hold values from -0.75 to 0.75
- w_gate_up: bfloat16 [1024, 9216], P('fsdp'), may hold values from -0.1875 to 0.1875
- w_down: bfloat16 [4608, 1024], P('fsdp'), may hold values from -0.09375 to 0.09375
- g_attn: bfloat16 [1024], P('fsdp'), may hold values from 0.099609375 to 1.8984375
- g_query: bfloat16 [64], P('fsdp'), may hold values from 0.099609375 to 1.8984375
- g_key: bfloat16 [64], P('fsdp'), may hold values from 0.099609375 to 1.8984375
- g_ffn: bfloat16 [1024], P('fsdp'), may hold values from 0.099609375 to 1.8984375
Outputs:
- output: float32 [4096, 1024], P(('rep', 'fsdp'))
- grad_tokens: float32 [4096, 1024], P(('rep', 'fsdp'))
- grad_w_qkv: float32 [1024, 2048], P('fsdp')
- grad_w_out: float32 [1024, 1024], P('fsdp')
- grad_w_gate_up: float32 [1024, 9216], P('fsdp')
- grad_w_down: float32 [4608, 1024], P('fsdp')
- grad_g_attn: float32 [1024], P('fsdp')
- grad_g_query: float32 [64], P('fsdp')
- grad_g_key: float32 [64], P('fsdp')
- grad_g_ffn: float32 [1024], P('fsdp')
Inputs may be any that keep to these rules, and one draw needn't show every extreme that they name: `segment_ids`: segment numbers never fall along the tokens; a segment holds 1 to 1024 tokens and one holds exactly 1024.
All inputs are finite; a program needn't handle non-finite values.
Results may differ from a plain program's by a relative error of at most 0.024.
Values may be sent and summed in bfloat16 or wider, within the bound.
A program may use at most 192 MiB of HBM per device.

v0:
```python
import jax
import jax.numpy as jnp
from jax import lax
from jax.sharding import PartitionSpec as P

QUERY_HEADS = 16
KEY_VALUE_HEADS = 8
HEAD_SIZE = 64
FF = 4608
NORM_EPS = 1e-05
ROPE_BASE = 1000000.0
MASK_FILL = -1e30


def rms_forward(values, gain_vec):
    inv_rms = lax.rsqrt(jnp.mean(values * values, axis=-1, keepdims=True) + NORM_EPS)
    return (values * inv_rms * gain_vec, inv_rms)


def root_mean_square_reverse(values, inv_rms, gain_vec, grad_out):
    weighted = grad_out * gain_vec
    grad_values = inv_rms * weighted - values * inv_rms**3 * jnp.mean(
        weighted * values, axis=-1, keepdims=True
    )
    grad_gain = jnp.sum((grad_out * values * inv_rms).reshape(-1, values.shape[-1]), axis=0)
    return (grad_values, grad_gain)


def rope_tables(positions, head_width):
    half_width = head_width // 2
    freqs_base = ROPE_BASE ** (-2.0 * jnp.arange(half_width, dtype=jnp.float32) / head_width)
    angles = positions.astype(jnp.float32)[:, None] * freqs_base[None, :]
    return (jnp.cos(angles)[:, None, :], jnp.sin(angles)[:, None, :])


def rotary_embed_apply(values, rotary_cosine, rotary_sine):
    half_width = values.shape[-1] // 2
    first_half = values[..., :half_width]
    second_half = values[..., half_width:]
    return jnp.concatenate(
        [
            first_half * rotary_cosine - second_half * rotary_sine,
            second_half * rotary_cosine + first_half * rotary_sine,
        ],
        axis=-1,
    )


def rotary_embed_invert(grad_out, rotary_cosine, rotary_sine):
    half_width = grad_out.shape[-1] // 2
    first_half = grad_out[..., :half_width]
    second_half = grad_out[..., half_width:]
    return jnp.concatenate(
        [
            first_half * rotary_cosine + second_half * rotary_sine,
            second_half * rotary_cosine - first_half * rotary_sine,
        ],
        axis=-1,
    )


def score_block(query_lowprec, key_lowprec, attention_mask_matrix):
    scale_dot = query_lowprec.shape[-1] ** (-0.5)
    scores = (
        jnp.einsum("qkgd,tkd->kgqt", query_lowprec, key_lowprec, preferred_element_type=jnp.float32)
        * scale_dot
    )
    return jnp.where(attention_mask_matrix, scores, MASK_FILL)


def attend_forward(query_lowprec, key_lowprec, value_lowprec, attention_mask_matrix):
    scores = score_block(query_lowprec, key_lowprec, attention_mask_matrix)
    top_score = jnp.max(scores, axis=-1, keepdims=True)
    expo_terms = jnp.where(attention_mask_matrix, jnp.exp(scores - top_score), 0.0)
    row_total = jnp.sum(expo_terms, axis=-1, keepdims=True)
    probs = (expo_terms / row_total).astype(jnp.bfloat16)
    mixed = jnp.einsum("kgqt,tkd->qkgd", probs, value_lowprec, preferred_element_type=jnp.float32)
    return (mixed.astype(jnp.bfloat16), top_score + jnp.log(row_total))


def attention_reverse_pass(
    query_lowprec,
    key_lowprec,
    value_lowprec,
    attention_mask_matrix,
    attention_lowprec,
    log_partition_sum,
    grad_attn,
):
    scale_dot = query_lowprec.shape[-1] ** (-0.5)
    scores = score_block(query_lowprec, key_lowprec, attention_mask_matrix)
    probs_again = jnp.where(attention_mask_matrix, jnp.exp(scores - log_partition_sum), 0.0)
    probs_low = probs_again.astype(jnp.bfloat16)
    value_gradient_rows = jnp.einsum(
        "kgqt,qkgd->tkd", probs_low, grad_attn, preferred_element_type=jnp.float32
    )
    d_probs = jnp.einsum(
        "qkgd,tkd->kgqt", grad_attn, value_lowprec, preferred_element_type=jnp.float32
    )
    delta_rows = jnp.sum(
        grad_attn.astype(jnp.float32) * attention_lowprec.astype(jnp.float32), axis=-1
    )
    delta_rows = jnp.transpose(delta_rows, (1, 2, 0))[..., None]
    d_score = (probs_again * (d_probs - delta_rows) * scale_dot).astype(jnp.bfloat16)
    grad_query = jnp.einsum(
        "kgqt,tkd->qkgd", d_score, key_lowprec, preferred_element_type=jnp.float32
    )
    grad_key = jnp.einsum(
        "kgqt,qkgd->tkd", d_score, query_lowprec, preferred_element_type=jnp.float32
    )
    return (grad_query, grad_key, value_gradient_rows)


def tdot(left_arr, right_arr):
    return lax.dot_general(
        left_arr, right_arr, (((0,), (0,)), ((), ())), preferred_element_type=jnp.float32
    )


def transposed_product(left_arr, right_arr):
    return lax.dot_general(
        left_arr, right_arr, (((1,), (1,)), ((), ())), preferred_element_type=jnp.float32
    )


def body(
    tokens, segment_ids, cotangent, w_qkv, w_out, w_gate_up, w_down, g_attn, g_query, g_key, g_ffn
):
    local_rows = tokens.shape[0]
    cluster_size = QUERY_HEADS // KEY_VALUE_HEADS
    seq_devices = lax.axis_size("fsdp")
    cluster_rows = seq_devices * local_rows
    member = lax.axis_index("fsdp")
    own_group = member * local_rows
    group_start = lax.axis_index("rep") * cluster_rows
    own_global = group_start + own_group
    key_value_width = KEY_VALUE_HEADS * HEAD_SIZE
    shards = (w_qkv, w_out, w_gate_up, w_down, g_attn, g_query, g_key, g_ffn)
    collected_rows = (
        lax.all_gather(shards[0], "fsdp", axis=0, tiled=True),
        lax.all_gather(shards[1], "fsdp", axis=0, tiled=True),
        lax.all_gather(shards[2], "fsdp", axis=0, tiled=True),
        lax.all_gather(shards[3], "fsdp", axis=0, tiled=True),
        lax.all_gather(shards[4], "fsdp", axis=0, tiled=True),
        lax.all_gather(shards[5], "fsdp", axis=0, tiled=True),
        lax.all_gather(shards[6], "fsdp", axis=0, tiled=True),
        lax.all_gather(shards[7], "fsdp", axis=0, tiled=True),
    )
    gain_sequence = [gain_arr.astype(jnp.float32) for gain_arr in collected_rows[4:]]
    query_seg = lax.dynamic_slice_in_dim(segment_ids, own_global, local_rows)
    key_seg = lax.dynamic_slice_in_dim(segment_ids, group_start, cluster_rows)
    query_pos = own_group + jnp.arange(local_rows, dtype=jnp.int32)
    key_pos = jnp.arange(cluster_rows, dtype=jnp.int32)
    attention_mask_matrix = (key_pos[None, :] <= query_pos[:, None]) & (
        query_seg[:, None] == key_seg[None, :]
    )
    rotary_cosine, rotary_sine = rope_tables(query_pos, HEAD_SIZE)
    normed_f, inv_in = rms_forward(tokens, gain_sequence[0])
    normed_in = normed_f.astype(jnp.bfloat16)
    projection_output = jnp.dot(normed_in, collected_rows[0], preferred_element_type=jnp.float32)
    query_raw = projection_output[:, : QUERY_HEADS * HEAD_SIZE].reshape(
        local_rows, QUERY_HEADS, HEAD_SIZE
    )
    key_unrotated = projection_output[
        :, QUERY_HEADS * HEAD_SIZE : (QUERY_HEADS + KEY_VALUE_HEADS) * HEAD_SIZE
    ].reshape(local_rows, KEY_VALUE_HEADS, HEAD_SIZE)
    value_lowprec = projection_output[:, (QUERY_HEADS + KEY_VALUE_HEADS) * HEAD_SIZE :].astype(
        jnp.bfloat16
    )
    query_norm_output, inv_query = rms_forward(query_raw, gain_sequence[1])
    key_norm, key_inverse_norm = rms_forward(key_unrotated, gain_sequence[2])
    query_lowprec = (
        rotary_embed_apply(query_norm_output, rotary_cosine, rotary_sine)
        .astype(jnp.bfloat16)
        .reshape(local_rows, KEY_VALUE_HEADS, cluster_size, HEAD_SIZE)
    )
    key_lowprec = rotary_embed_apply(key_norm, rotary_cosine, rotary_sine).astype(jnp.bfloat16)
    kv_pair = jnp.stack([key_lowprec.reshape(local_rows, key_value_width), value_lowprec])
    key_value_span = lax.all_gather(kv_pair, "fsdp", axis=1, tiled=True)
    span_keys = key_value_span[0].reshape(cluster_rows, KEY_VALUE_HEADS, HEAD_SIZE)
    span_values = key_value_span[1].reshape(cluster_rows, KEY_VALUE_HEADS, HEAD_SIZE)
    attention_lowprec, log_partition_sum = attend_forward(
        query_lowprec, span_keys, span_values, attention_mask_matrix
    )
    attn_flat = attention_lowprec.reshape(local_rows, QUERY_HEADS * HEAD_SIZE)
    mid_stream = tokens + jnp.dot(attn_flat, collected_rows[1], preferred_element_type=jnp.float32)
    normed_g, inv_mid = rms_forward(mid_stream, gain_sequence[3])
    normed_mid = normed_g.astype(jnp.bfloat16)
    gate_up = jnp.dot(normed_mid, collected_rows[2], preferred_element_type=jnp.float32)
    gate_part = gate_up[:, :FF]
    up_part = gate_up[:, FF:]
    sigmoid_gate = jax.nn.sigmoid(gate_part)
    hidden = (gate_part * sigmoid_gate * up_part).astype(jnp.bfloat16)
    output = mid_stream + jnp.dot(hidden, collected_rows[3], preferred_element_type=jnp.float32)
    cot_low = cotangent.astype(jnp.bfloat16)
    grad_down = tdot(hidden, cot_low)
    d_hidden = transposed_product(cot_low, collected_rows[3])
    d_gate = d_hidden * up_part * sigmoid_gate * (1.0 + gate_part * (1.0 - sigmoid_gate))
    d_up = d_hidden * gate_part * sigmoid_gate
    d_gate_up = jnp.concatenate([d_gate, d_up], axis=1).astype(jnp.bfloat16)
    grad_gate_up = tdot(normed_mid, d_gate_up)
    d_normed_mid = transposed_product(d_gate_up, collected_rows[2])
    back_mid, grad_ffn_gain = root_mean_square_reverse(
        mid_stream, inv_mid, gain_sequence[3], d_normed_mid
    )
    d_mid = cotangent + back_mid
    middle_cotangent_lowprec = d_mid.astype(jnp.bfloat16)
    grad_out_proj = tdot(attn_flat, middle_cotangent_lowprec)
    attention_cotangent = (
        transposed_product(middle_cotangent_lowprec, collected_rows[1])
        .astype(jnp.bfloat16)
        .reshape(local_rows, KEY_VALUE_HEADS, cluster_size, HEAD_SIZE)
    )
    query_lowprec_gradient, grad_kwin, grad_vwin = attention_reverse_pass(
        query_lowprec,
        span_keys,
        span_values,
        attention_mask_matrix,
        attention_lowprec,
        log_partition_sum,
        attention_cotangent,
    )
    kv_grads = jnp.stack(
        [
            grad_kwin.reshape(cluster_rows, key_value_width),
            grad_vwin.reshape(cluster_rows, key_value_width),
        ]
    )
    local_key_value = lax.psum_scatter(
        kv_grads.astype(jnp.bfloat16), "fsdp", scatter_dimension=1, tiled=True
    ).astype(jnp.float32)
    d_query, grad_query_gain = root_mean_square_reverse(
        query_raw,
        inv_query,
        gain_sequence[1],
        rotary_embed_invert(
            query_lowprec_gradient.reshape(local_rows, QUERY_HEADS, HEAD_SIZE),
            rotary_cosine,
            rotary_sine,
        ),
    )
    key_cotangent, key_gain_gradient = root_mean_square_reverse(
        key_unrotated,
        key_inverse_norm,
        gain_sequence[2],
        rotary_embed_invert(
            local_key_value[0].reshape(local_rows, KEY_VALUE_HEADS, HEAD_SIZE),
            rotary_cosine,
            rotary_sine,
        ),
    )
    d_projected = jnp.concatenate(
        [
            d_query.reshape(local_rows, -1),
            key_cotangent.reshape(local_rows, -1),
            local_key_value[1],
        ],
        axis=1,
    ).astype(jnp.bfloat16)
    grad_qkv = tdot(normed_in, d_projected)
    d_normed_in = transposed_product(d_projected, collected_rows[0])
    back_in, grad_attn_gain = root_mean_square_reverse(
        tokens, inv_in, gain_sequence[0], d_normed_in
    )
    grad_tokens = d_mid + back_in
    grads_local = (
        grad_qkv,
        grad_out_proj,
        grad_gate_up,
        grad_down,
        grad_attn_gain,
        grad_query_gain,
        key_gain_gradient,
        grad_ffn_gain,
    )
    grad_share = (
        lax.psum_scatter(
            grads_local[0].astype(jnp.bfloat16), "fsdp", scatter_dimension=0, tiled=True
        ).astype(jnp.float32),
        lax.psum_scatter(
            grads_local[1].astype(jnp.bfloat16), "fsdp", scatter_dimension=0, tiled=True
        ).astype(jnp.float32),
        lax.psum_scatter(
            grads_local[2].astype(jnp.bfloat16), "fsdp", scatter_dimension=0, tiled=True
        ).astype(jnp.float32),
        lax.psum_scatter(
            grads_local[3].astype(jnp.bfloat16), "fsdp", scatter_dimension=0, tiled=True
        ).astype(jnp.float32),
        lax.psum_scatter(
            grads_local[4].astype(jnp.bfloat16), "fsdp", scatter_dimension=0, tiled=True
        ).astype(jnp.float32),
        lax.psum_scatter(
            grads_local[5].astype(jnp.bfloat16), "fsdp", scatter_dimension=0, tiled=True
        ).astype(jnp.float32),
        lax.psum_scatter(
            grads_local[6].astype(jnp.bfloat16), "fsdp", scatter_dimension=0, tiled=True
        ).astype(jnp.float32),
        lax.psum_scatter(
            grads_local[7].astype(jnp.bfloat16), "fsdp", scatter_dimension=0, tiled=True
        ).astype(jnp.float32),
    )
    grad_total = (
        lax.psum(grad_share[0].astype(jnp.bfloat16), "rep").astype(jnp.float32),
        lax.psum(grad_share[1].astype(jnp.bfloat16), "rep").astype(jnp.float32),
        lax.psum(grad_share[2].astype(jnp.bfloat16), "rep").astype(jnp.float32),
        lax.psum(grad_share[3].astype(jnp.bfloat16), "rep").astype(jnp.float32),
        lax.psum(grad_share[4].astype(jnp.bfloat16), "rep").astype(jnp.float32),
        lax.psum(grad_share[5].astype(jnp.bfloat16), "rep").astype(jnp.float32),
        lax.psum(grad_share[6].astype(jnp.bfloat16), "rep").astype(jnp.float32),
        lax.psum(grad_share[7].astype(jnp.bfloat16), "rep").astype(jnp.float32),
    )
    return (
        output,
        grad_tokens,
        grad_total[0],
        grad_total[1],
        grad_total[2],
        grad_total[3],
        grad_total[4],
        grad_total[5],
        grad_total[6],
        grad_total[7],
    )


def solution(mesh):
    placed = (
        P(("rep", "fsdp"), None),
        P(),
        P(("rep", "fsdp"), None),
        P("fsdp", None),
        P("fsdp", None),
        P("fsdp", None),
        P("fsdp", None),
        P("fsdp"),
        P("fsdp"),
        P("fsdp"),
        P("fsdp"),
    )
    return jax.shard_map(
        body,
        mesh=mesh,
        in_specs=placed,
        out_specs=(
            P(("rep", "fsdp"), None),
            P(("rep", "fsdp"), None),
            P("fsdp", None),
            P("fsdp", None),
            P("fsdp", None),
            P("fsdp", None),
            P("fsdp"),
            P("fsdp"),
            P("fsdp"),
            P("fsdp"),
        ),
        check_vma=False,
    )
```

profile of v0, /device:TPU:0, one launch (start us, length us, event | category | flops | bytes accessed | tf_op | source)
XLA Modules:
  0.0 968.5 jit_solution(10914518348454304523)
XLA Ops:
  8.0 13.6 %all-gather = bf16[8,1,128]{2,1,0:T(2,128)(2,1)S(1)} all-gather(bf16[1,1,128]{2,1,0:T(2,128)(2,1)} %bitcast.157), channel_id=1, replica_groups=mesh['rep'=4,'fsdp'=8] {'fsdp'}, dimensions={0}, use_global_device_ids=true | all-gather | bytes 2304 | tf_op jit(solution)/shard_map/all_gather | solution.py:144
  25.3 15.0 %all-reduce.7 = (bf16[64]{0:T(256)(128)(2,1)S(1)}, bf16[64]{0:T(256)(128)(2,1)S(1)}) all-reduce(bf16[64]{0:T(256)(128)(2,1)S(1)} %dynamic-update-slice, bf16[64]{0:T(256)(128)(2,1)S(1)} %dynamic-update-slice.1), channel_id=1, replica_groups=mesh['rep'=4,'fsdp'=8] {'fsdp'}, use_global_device_ids=true, to_apply=%add | all-reduce | flops 128 | bytes 512
  42.8 16.7 %all-gather.8.cloned.1.call-done = bf16[1024,2048]{1,0:T(8,128)(2,1)} async-done(((bf16[128,2048]{1,0:T(8,128)(2,1)}), bf16[1024,2048]{1,0:T(8,128)(2,1)}) %all-gather.8.cloned.1.call-update) | async-done | bytes 4194320 | tf_op jit(solution)/shard_map/all_gather | solution.py:140
  59.5 3.1 fusion.40
  68.1 10.1 %all-gather.1 = bf16[8,1,128]{2,1,0:T(2,128)(2,1)S(1)} all-gather(bf16[1,1,128]{2,1,0:T(2,128)(2,1)S(1)} %bitcast.158), channel_id=1, replica_groups=mesh['rep'=4,'fsdp'=8] {'fsdp'}, dimensions={0}, use_global_device_ids=true | all-gather | bytes 2304 | tf_op jit(solution)/shard_map/all_gather | solution.py:147
  79.7 13.1 %all-gather.10.cloned.1.call-done = bf16[2,1024,512]{2,1,0:T(8,128)(2,1)} async-done(((bf16[2,128,512]{2,1,0:T(8,128)(2,1)}), bf16[2,1024,512]{2,1,0:T(8,128)(2,1)}) %all-gather.10.cloned.1.call-update) | async-done | bytes 2097168 | tf_op jit(solution)/shard_map/all_gather | solution.py:179
  92.8 2.6 fusion.42
  105.7 17.3 %all-gather.12.cloned.1.call-done = bf16[1024,1024]{1,0:T(8,128)(2,1)} async-done(((bf16[128,1024]{1,0:T(8,128)(2,1)}), bf16[1024,1024]{1,0:T(8,128)(2,1)}) %all-gather.12.cloned.1.call-update) | async-done | bytes 2097168 | tf_op jit(solution)/shard_map/all_gather | solution.py:141
  126.3 165.9 %all-gather.14.cloned.1.call-done = bf16[1024,9216]{1,0:T(8,128)(2,1)} async-done(((bf16[128,9216]{1,0:T(8,128)(2,1)}), bf16[1024,9216]{1,0:T(8,128)(2,1)}) %all-gather.14.cloned.1.call-update) | async-done | bytes 18874384 | tf_op jit(solution)/shard_map/all_gather | solution.py:142
  292.2 11.3 %fusion.41 = f32[128,9216]{1,0:T(8,128)} fusion(bf16[1024,9216]{1,0:T(8,128)(2,1)} %all-gather.14.cloned.1.call-done, f32[128,1024]{1,0:T(8,128)S(1)} %get-tuple-element.62, f32[1024]{0:T(1024)S(1)} %bitcast.143, f32[128]{0:T(128)S(1)} %get-tuple-element.58), kind=kOutput, calls=%fused_computation.114 | convolution fusion | flops 2416312320 | bytes 24121856 | tf_op jit(solution)/shard_map/dot_general | solution.py:189
  303.5 79.1 %all-gather.16.cloned.1.call-done = bf16[4608,1024]{1,0:T(8,128)(2,1)} async-done(((bf16[576,1024]{1,0:T(8,128)(2,1)}), bf16[4608,1024]{1,0:T(8,128)(2,1)}) %all-gather.16.cloned.1.call-update) | async-done | bytes 9437200 | tf_op jit(solution)/shard_map/all_gather | solution.py:143
  382.6 8.9 multiply_convert_fusion.1
  391.6 12.6 %multiply_reduce_fusion = (bf16[1024]{0:T(1024)(128)(2,1)}, f32[128]{0:T(128)S(1)}, f32[128,1024]{1,0:T(8,128)S(1)}) fusion(f32[128,1024]{1,0:T(8,128)S(1)} %get-tuple-element.62, f32[128]{0:T(128)S(1)} %copy-done.47, f32[1024]{0:T(1024)S(1)} %bitcast.144, bf16[1024,9216]{1,0:T(8,128)(2,1)} %all-gather.14.cloned.1.call-done, ...), kind=kOutput, calls=%fused_computation.39 | convolution fusion | flops 2421423104 | bytes 22289408 | tf_op jit(solution)/shard_map/dot_general | solution.py:121
  409.7 6.5 bitcast_convert_fusion
  416.3 5.7 fusion.2
  431.0 3.1 pad_maximum_fusion.1
  434.1 3.1 convolution_convert_fusion.3
  455.5 3.1 fusion.44
  478.4 4.4 convolution_convert_fusion.2
  483.8 5.1 convolution_convert_fusion.1
  489.6 10.9 %convolution_convert_fusion = bf16[1024,9216]{1,0:T(8,128)(2,1)} fusion(bf16[128,4608]{1,0:T(8,128)(2,1)} %copy-done.27, bf16[128,4608]{1,0:T(8,128)(2,1)} %copy-done.26, f32[128,1024]{1,0:T(8,128)S(1)} %get-tuple-element.62, f32[1024]{0:T(1024)S(1)} %bitcast.146, f32[128]{0:T(128)S(1)} %copy-done.48), kind=kOutput, calls=%fused_computation | convolution fusion | flops 2430468096 | bytes 21762560 | tf_op jit(solution)/shard_map/dot_general | solution.py:115
  500.8 4.7 reduce-scatter.10.cloned.1.call-done
  505.5 51.2 %reduce-scatter.8.cloned.1.call-done = bf16[128,2048]{1,0:T(8,128)(2,1)} async-done(((bf16[1024,2048]{1,0:T(8,128)(2,1)}), bf16[128,2048]{1,0:T(8,128)(2,1)}) %reduce-scatter.8.cloned.1.call-update) | async-done | bytes 524304 | tf_op jit(solution)/shard_map/reduce_scatter | solution.py:277
  556.7 100.2 %reduce-scatter.14.cloned.1.call-done = bf16[576,1024]{1,0:T(8,128)(2,1)} async-done(((bf16[4608,1024]{1,0:T(8,128)(2,1)}), bf16[576,1024]{1,0:T(8,128)(2,1)}) %reduce-scatter.14.cloned.1.call-update) | async-done | bytes 1179664 | tf_op jit(solution)/shard_map/reduce_scatter | solution.py:286
  657.0 188.6 %reduce-scatter.12.cloned.1.call-done = bf16[128,9216]{1,0:T(8,128)(2,1)} async-done(((bf16[1024,9216]{1,0:T(8,128)(2,1)}), bf16[128,9216]{1,0:T(8,128)(2,1)}) %reduce-scatter.12.cloned.1.call-update) | async-done | bytes 2359312 | tf_op jit(solution)/shard_map/reduce_scatter | solution.py:283
  852.3 3.3 fusion.15
  855.5 5.9 convolution_add_fusion.1
  863.5 4.0 multiply_reduce_fusion.1
  867.5 14.3 %all-reduce.6 = (bf16[1024]{0:T(1024)(128)(2,1)S(1)}, bf16[64]{0:T(256)(128)(2,1)S(1)}, bf16[64]{0:T(256)(128)(2,1)S(1)}, bf16[1024]{0:T(1024)(128)(2,1)S(1)}) all-reduce(bf16[1024]{0:T(1024)(128)(2,1)S(1)} %get-tuple-element.12, bf16[64]{0:T(256)(128)(2,1)S(1)} %copy-done.56, ...), channel_id=7, replica_groups=mesh['rep'=4,'fsdp'=8] {'fsdp'}, use_global_device_ids=true, to_apply=%region_21.22.clone | all-reduce | flops 2176 | bytes 8704
  882.0 10.3 %all-reduce.8 = (bf16[128]{0:T(256)(128)(2,1)S(1)}, bf16[8]{0:T(256)(128)(2,1)S(1)}, bf16[8]{0:T(256)(128)(2,1)S(1)}, bf16[128]{0:T(256)(128)(2,1)S(1)}) all-reduce(bf16[128]{0:T(256)(128)(2,1)S(1)} %dynamic-slice.3, bf16[8]{0:T(256)(128)(2,1)S(1)} %dynamic-slice.5, ...), channel_id=1, replica_groups=mesh['rep'=4,'fsdp'=8] {'rep'}, use_global_device_ids=true, to_apply=%region_22.23 | all-reduce | flops 272 | bytes 1088 | tf_op jit(solution)/shard_map/psum | solution.py:307
  895.4 58.3 %all-reduce.12.cloned.1.call-done = (bf16[128,2048]{1,0:T(8,128)(2,1)}, bf16[128,1024]{1,0:T(8,128)(2,1)}, bf16[128,9216]{1,0:T(8,128)(2,1)}, bf16[576,1024]{1,0:T(8,128)(2,1)}) async-done(((bf16[128,2048]{1,0:T(8,128)(2,1)}, bf16[128,1024]{1,0:T(8,128)(2,1)}, bf16[128,9216]{1,0:T(8,128)(2,1)}, bf16[576,1024]{1,0:T(8,128)(2,1)}), (bf16[128,2048]{1,0:T(8,128)(2,1)}, bf16[128,1024]{1,0:T(8,128)(2,1)}, ...) | async-done | bytes 4325392 | tf_op jit(solution)/shard_map/psum | solution.py:303
  953.7 4.4 convert_element_type.164
  (249 shorter events, 95.0 us)
Async XLA Ops:
  7.2 52.3 %all-gather.8.cloned.1.call-start = ((), (), s32[]{:S(2)}) async-start(), calls=%async_computation.5 | async-start | bytes 4718592 | tf_op jit(solution)/shard_map/all_gather | solution.py:140
  7.9 84.9 %all-gather.10.cloned.1.call-start = ((), (), s32[]{:S(2)}) async-start(), calls=%async_computation.6 | async-start | bytes 2359296 | tf_op jit(solution)/shard_map/all_gather | solution.py:179
  40.3 26.4 %copy-start.61 = (bf16[64]{0:T(256)(128)(2,1)}, bf16[64]{0:T(256)(128)(2,1)S(1)}, u32[]{:S(2)}) copy-start(bf16[64]{0:T(256)(128)(2,1)S(1)} %get-tuple-element.19) | copy-start | bytes 388
  40.3 23.4 %copy-start.55 = (f32[64]{0:T(128)}, f32[64]{0:T(128)S(1)}, u32[]{:S(2)}) copy-start(f32[64]{0:T(128)S(1)} %convert_element_type.142) | copy-start | bytes 772
  42.6 20.1 %copy-start.50 = (f32[128]{0:T(128)}, f32[128]{0:T(128)S(1)}, u32[]{:S(2)}) copy-start(f32[128]{0:T(128)S(1)} %get-tuple-element.56) | copy-start | bytes 1540
  42.8 36.8 %copy-start.39 = (f32[128,32]{0,1:T(8,128)}, f32[128,32]{0,1:T(8,128)S(1)}, u32[]{:S(2)}) copy-start(f32[128,32]{0,1:T(8,128)S(1)} %get-tuple-element.51) | copy-start | bytes 49156
  42.8 36.8 %copy-start.41 = (f32[128,32]{0,1:T(8,128)}, f32[128,32]{0,1:T(8,128)S(1)}, u32[]{:S(2)}) copy-start(f32[128,32]{0,1:T(8,128)S(1)} %get-tuple-element.52) | copy-start | bytes 49156
  62.6 15.8 %copy-start.8 = (f32[128,2048]{1,0:T(8,128)}, f32[128,2048]{1,0:T(8,128)S(1)}, u32[]{:S(2)}) copy-start(f32[128,2048]{1,0:T(8,128)S(1)} %fusion.40) | copy-start | bytes 3145732
  64.7 58.3 %all-gather.12.cloned.1.call-start = ((), (), s32[]{:S(2)}) async-start(), calls=%async_computation.7 | async-start | bytes 2359296 | tf_op jit(solution)/shard_map/all_gather | solution.py:141
  65.4 226.8 %all-gather.14.cloned.1.call-start = ((), (), s32[]{:S(2)}) async-start(), calls=%async_computation.8 | async-start | bytes 21233664 | tf_op jit(solution)/shard_map/all_gather | solution.py:142
  66.0 316.6 %all-gather.16.cloned.1.call-start = ((), (), s32[]{:S(2)}) async-start(), calls=%async_computation.9 | async-start | bytes 10616832 | tf_op jit(solution)/shard_map/all_gather | solution.py:143
  66.6 402.0 %reduce-scatter.6.cloned.1.call-start = ((), (), s32[]{:S(2)}) async-start(), calls=%async_computation.10 | async-start | bytes 2359296 | tf_op jit(solution)/shard_map/reduce_scatter | solution.py:229
  66.7 28.8 %copy-start.52 = (f32[64]{0:T(128)}, f32[64]{0:T(128)S(1)}, u32[]{:S(2)}) copy-start(f32[64]{0:T(128)S(1)} %convert_element_type.145) | copy-start | bytes 772
  78.4 23.3 %copy-start.20 = (pred[128,1024]{0,1:T(8,128)(4,1)}, pred[128,1024]{0,1:T(8,128)(4,1)S(1)}, u32[]{:S(2)}) copy-start(pred[128,1024]{0,1:T(8,128)(4,1)S(1)} %fusion.18) | copy-start | bytes 393220
  78.5 17.0 %copy-start.10 = (f32[128,1024]{1,0:T(8,128)}, f32[128,1024]{1,0:T(8,128)S(1)}, u32[]{:S(2)}) copy-start(f32[128,1024]{1,0:T(8,128)S(1)} %slice.77) | copy-start | bytes 1572868
  78.7 18.3 %copy-start.4 = (f32[128,1024]{0,1:T(8,128)}, f32[128,1024]{0,1:T(8,128)S(1)}, u32[]{:S(2)}) copy-start(f32[128,1024]{0,1:T(8,128)S(1)} %copy.98) | copy-start | bytes 1572868
  79.7 18.6 %copy-start.22 = (bf16[128,16,32]{0,2,1:T(8,128)(2,1)}, bf16[128,16,32]{0,2,1:T(8,128)(2,1)S(1)}, u32[]{:S(2)}) copy-start(bf16[128,16,32]{0,2,1:T(8,128)(2,1)S(1)} %get-tuple-element.35) | copy-start | bytes 393220
  79.7 18.6 %copy-start.24 = (bf16[128,16,32]{0,2,1:T(8,128)(2,1)}, bf16[128,16,32]{0,2,1:T(8,128)(2,1)S(1)}, u32[]{:S(2)}) copy-start(bf16[128,16,32]{0,2,1:T(8,128)(2,1)S(1)} %get-tuple-element.36) | copy-start | bytes 393220
  103.1 19.9 %copy-start.2 = (f32[128,1024]{1,0:T(8,128)S(1)}, f32[128,1024]{1,0:T(8,128)}, u32[]{:S(2)}) copy-start(f32[128,1024]{1,0:T(8,128)} %param.11) | copy-start | bytes 1572868
  105.7 197.9 %copy-start.17 = (bf16[8,64,2,128]{3,1,2,0:T(8,128)(2,1)}, bf16[8,64,2,128]{3,1,2,0:T(8,128)(2,1)S(1)}, u32[]{:S(2)}) copy-start(bf16[8,64,2,128]{3,1,2,0:T(8,128)(2,1)S(1)} %fusion.13) | copy-start | bytes 786436
  125.7 177.8 %copy-start.46 = (f32[128]{0:T(128)}, f32[128]{0:T(128)S(1)}, u32[]{:S(2)}) copy-start(f32[128]{0:T(128)S(1)} %get-tuple-element.58) | copy-start | bytes 1540
  434.0 71.5 %reduce-scatter.10.cloned.1.call-start = ((), (), s32[]{:S(2)}) async-start(), calls=%async_computation.12 | async-start | bytes 2359296 | tf_op jit(solution)/shard_map/reduce_scatter | solution.py:280
  437.2 119.5 %reduce-scatter.8.cloned.1.call-start = ((), (), s32[]{:S(2)}) async-start(), calls=%async_computation.11 | async-start | bytes 4718592 | tf_op jit(solution)/shard_map/reduce_scatter | solution.py:277
  482.8 174.2 %reduce-scatter.14.cloned.1.call-start = ((), (), s32[]{:S(2)}) async-start(), calls=%async_computation.14 | async-start | bytes 10616832 | tf_op jit(solution)/shard_map/reduce_scatter | solution.py:286
  488.9 356.6 %reduce-scatter.12.cloned.1.call-start = ((), (), s32[]{:S(2)}) async-start(), calls=%async_computation.13 | async-start | bytes 21233664 | tf_op jit(solution)/shard_map/reduce_scatter | solution.py:283
  500.5 346.5 %copy-start.11 = (f32[128,1024]{1,0:T(8,128)S(1)}, f32[128,1024]{1,0:T(8,128)}, u32[]{:S(2)}) copy-start(f32[128,1024]{1,0:T(8,128)} %copy-done.10) | copy-start | bytes 1572868
  500.5 347.7 %copy-start.45 = (f32[128,8]{0,1:T(8,128)S(1)}, f32[128,8]{0,1:T(8,128)}, u32[]{:S(2)}) copy-start(f32[128,8]{0,1:T(8,128)} %copy-done.44) | copy-start | bytes 12292
  500.5 347.8 %copy-start.13 = (f32[128,512]{1,0:T(8,128)S(1)}, f32[128,512]{1,0:T(8,128)}, u32[]{:S(2)}) copy-start(f32[128,512]{1,0:T(8,128)} %copy-done.12) | copy-start | bytes 786436
  500.5 350.4 %copy-start.15 = (f32[128,16,32]{0,2,1:T(8,128)S(1)}, f32[128,16,32]{0,2,1:T(8,128)}, u32[]{:S(2)}) copy-start(f32[128,16,32]{0,2,1:T(8,128)} %copy-done.14) | copy-start | bytes 786436
  500.6 453.1 %all-reduce.12.cloned.1.call-start = ((), (), s32[]{:S(2)}) async-start(), calls=%async_computation.15 | async-start | bytes 8650752 | tf_op jit(solution)/shard_map/psum | solution.py:303
  861.7 32.7 %copy-start.7 = (f32[128,1024]{1,0:T(8,128)S(1)}, f32[128,1024]{1,0:T(8,128)}, u32[]{:S(2)}) copy-start(f32[128,1024]{1,0:T(8,128)} %copy-done.6) | copy-start | bytes 1572868
  861.7 32.7 %copy-start.57 = (f32[128]{0:T(128)S(1)}, f32[128]{0:T(128)}, u32[]{:S(2)}) copy-start(f32[128]{0:T(128)} %get-tuple-element.55) | copy-start | bytes 1540
  (41 other events, 229.0 us)
Sparse Core Ops, SparseCore 0:
  9.6 49.8 all-gather.7
  64.8 27.9 all-gather.9
  94.4 28.5 all-gather.11
  124.5 167.6 all-gather.13
  293.7 88.8 all-gather.15
  434.1 34.4 reduce-scatter.5
  470.9 34.5 reduce-scatter.9
  508.4 48.2 reduce-scatter.7
  559.0 97.8 reduce-scatter.13
  659.2 186.3 reduce-scatter.11
  849.3 104.2 all-reduce.11
where the time goes:
time: 972 us; the launch traced here: 968 us
  waiting for transfers between devices  699 us (72%)
  matrix products  94.7 us (10%)
  blocking collectives  63.3 us (7%)
  local copies, waits for them, and re-layouts  56.8 us (6%)
  other arithmetic  36.6 us (4%)
  between operations  16.9 us (2%)
    reduce_scatter x1, waiting for transfers between devices, body(): lax.psum_scatter(grads_local[2].astype(jnp.bfloat16), 'fsdp', scatter_dim...  189 us
    all_gather x1, waiting for transfers between devices, body(): lax.all_gather(shards[2], 'fsdp', axis=0, tiled=True)  166 us
    reduce_scatter x1, waiting for transfers between devices, body(): lax.psum_scatter(grads_local[3].astype(jnp.bfloat16), 'fsdp', scatter_dim...  100 us
    all_gather x1, waiting for transfers between devices, body(): lax.all_gather(shards[3], 'fsdp', axis=0, tiled=True)  79.1 us
    psum x1, waiting for transfers between devices, body(): lax.psum(grad_share[0].astype(jnp.bfloat16), 'rep').astype(jnp.float32)  58.3 us
    reduce_scatter x1, waiting for transfers between devices, body(): lax.psum_scatter(grads_local[0].astype(jnp.bfloat16), 'fsdp', scatter_dim...  51.2 us
    unnamed x2, blocking collectives  29.3 us
    dot_general x4, matrix products, transposed_product(): lax.dot_general(left_arr, right_arr, (((1,), (1,)), ((), ())), preferred_...  27 us
  transfers between devices with their start and end apart: 11, of which 11 were waited for; matrix products, arithmetic and copies ran while one was open for 12% of the time, Pallas kernels for 0%

commit v1 on v0

--- a/solution.py
+++ b/solution.py
@@ -10,6 +10,18 @@
 NORM_EPS = 1e-05
 ROPE_BASE = 1000000.0
 MASK_FILL = -1e30
+
+
+def doubled_up(array, axis, dim):
+    ways, here, hop = (lax.axis_size(axis), lax.axis_index(axis), array.shape[dim])
+    line, have = (array, 1)
+    while have < ways:
+        line = jnp.concatenate(
+            [line, lax.ppermute(line, axis, [(d, (d - have) % ways) for d in range(ways)])],
+            axis=dim,
+        )
+        have = 2 * have
+    return jnp.roll(line, here * hop, axis=dim)
 
 
 def rms_forward(values, gain_vec):
@@ -140,7 +152,7 @@
         lax.all_gather(shards[0], "fsdp", axis=0, tiled=True),
         lax.all_gather(shards[1], "fsdp", axis=0, tiled=True),
         lax.all_gather(shards[2], "fsdp", axis=0, tiled=True),
-        lax.all_gather(shards[3], "fsdp", axis=0, tiled=True),
+        doubled_up(shards[3], "fsdp", 0),
         lax.all_gather(shards[4], "fsdp", axis=0, tiled=True),
         lax.all_gather(shards[5], "fsdp", axis=0, tiled=True),
         lax.all_gather(shards[6], "fsdp", axis=0, tiled=True),

time: 972 us -> 1170 us (1.20)
  blocking collectives: 63.3 us -> 243 us
    ppermute x0 -> x3, waiting for transfers between devices: none -> 254 us  [doubled_up(): lax.ppermute(line, axis, [(d, (d - have) % ways) for d in range(ways)])]
    all_gather x1, blocking collectives: 10.1 us -> 189 us  [body(): lax.all_gather(shards[7], 'fsdp', axis=0, tiled=True)]
    all_gather x1, waiting for transfers between devices: 166 us -> 0.01 us  [body(): lax.all_gather(shards[2], 'fsdp', axis=0, tiled=True)]
    all_gather x1 -> x0, waiting for transfers between devices: 79.1 us -> none  [body(): lax.all_gather(shards[3], 'fsdp', axis=0, tiled=True)]
    reduce_scatter x1, waiting for transfers between devices: 1.6 us -> 33.2 us  [body(): lax.psum_scatter(kv_grads.astype(jnp.bfloat16), 'fsdp', scatter_dimension...]
    all_gather x1, waiting for transfers between devices: 17.3 us -> 0.02 us  [body(): lax.all_gather(shards[1], 'fsdp', axis=0, tiled=True)]
    all_gather x1, waiting for transfers between devices: 13.1 us -> 0.01 us  [body(): key_value_span = lax.all_gather(kv_pair, 'fsdp', axis=1, tiled=True)]
    unnamed x133 -> x128, local copies, waits for them, and re-layouts: 10.5 us -> 23.3 us
  transfers between devices with their start and end apart: 11 -> 13, of which waited for: 11 -> 10; matrix products, arithmetic and copies ran while one was open for 12% -> 11% of each run, Pallas kernels for 0% -> 0%
where the time goes in v1:
time: 1170 us
  waiting for transfers between devices  710 us (61%)
  blocking collectives  243 us (21%)
  matrix products  93.5 us (8%)
  local copies, waits for them, and re-layouts  62.6 us (5%)
  other arithmetic  40.2 us (3%)
  between operations  17.1 us (1%)
    ppermute x3, waiting for transfers between devices, doubled_up(): lax.ppermute(line, axis, [(d, (d - have) % ways) for d in range(ways)])  254 us
    all_gather x1, blocking collectives, body(): lax.all_gather(shards[7], 'fsdp', axis=0, tiled=True)  189 us
    reduce_scatter x1, waiting for transfers between devices, body(): lax.psum_scatter(grads_local[2].astype(jnp.bfloat16), 'fsdp', scatter_dim...  189 us
    reduce_scatter x1, waiting for transfers between devices, body(): lax.psum_scatter(grads_local[3].astype(jnp.bfloat16), 'fsdp', scatter_dim...  100 us
    psum x1, waiting for transfers between devices, body(): lax.psum(grad_share[0].astype(jnp.bfloat16), 'rep').astype(jnp.float32)  58.6 us
    reduce_scatter x1, waiting for transfers between devices, body(): lax.psum_scatter(grads_local[0].astype(jnp.bfloat16), 'fsdp', scatter_dim...  51.4 us
    reduce_scatter x1, waiting for transfers between devices, body(): lax.psum_scatter(kv_grads.astype(jnp.bfloat16), 'fsdp', scatter_dimension...  33.2 us
    unnamed x2, blocking collectives  29.6 us
  transfers between devices with their start and end apart: 13, of which 10 were waited for; matrix products, arithmetic and copies ran while one was open for 11% of the time, Pallas kernels for 0%

profile of v1, /device:TPU:0, one launch (start us, length us, event | category | flops | bytes accessed | tf_op | source)
XLA Modules:
  0.0 1167.5 jit_solution(2503324477717165499)
XLA Ops:
  8.0 13.6 %all-gather = bf16[8,1,128]{2,1,0:T(2,128)(2,1)S(1)} all-gather(bf16[1,1,128]{2,1,0:T(2,128)(2,1)} %bitcast.157), channel_id=1, replica_groups=mesh['rep'=4,'fsdp'=8] {'fsdp'}, dimensions={0}, use_global_device_ids=true | all-gather | bytes 2304 | tf_op jit(solution)/shard_map/all_gather | solution.py:156
  25.3 15.0 %all-reduce.7 = (bf16[64]{0:T(256)(128)(2,1)S(1)}, bf16[64]{0:T(256)(128)(2,1)S(1)}) all-reduce(bf16[64]{0:T(256)(128)(2,1)S(1)} %dynamic-update-slice, bf16[64]{0:T(256)(128)(2,1)S(1)} %dynamic-update-slice.1), channel_id=1, replica_groups=mesh['rep'=4,'fsdp'=8] {'fsdp'}, use_global_device_ids=true, to_apply=%add | all-reduce | flops 128 | bytes 512
  42.3 17.3 %all-gather.7.cloned.1.call-done = bf16[1024,2048]{1,0:T(8,128)(2,1)} async-done(((bf16[128,2048]{1,0:T(8,128)(2,1)}), bf16[1024,2048]{1,0:T(8,128)(2,1)}) %all-gather.7.cloned.1.call-update) | async-done | bytes 4194320 | tf_op jit(solution)/shard_map/all_gather | solution.py:152
  59.5 3.2 fusion.51
  68.7 30.6 %collective-permute-done = bf16[576,1024]{1,0:T(8,128)(2,1)S(1)} collective-permute-done((bf16[576,1024]{1,0:T(8,128)(2,1)S(1)}, bf16[576,1024]{1,0:T(8,128)(2,1)S(1)}, u32[]{:S(2)}, u32[]{:S(2)}) %collective-permute-start) | collective-permute-done | bytes 1179680 | tf_op jit(solution)/shard_map/ppermute | solution.py:20
  99.5 71.0 %collective-permute-done.1 = bf16[1152,1024]{1,0:T(8,128)(2,1)S(1)} collective-permute-done((bf16[1152,1024]{1,0:T(8,128)(2,1)S(1)}, bf16[1152,1024]{1,0:T(8,128)(2,1)S(1)}, u32[]{:S(2)}, u32[]{:S(2)}) %collective-permute-start.1) | collective-permute-done | bytes 2359328 | tf_op jit(solution)/shard_map/ppermute | solution.py:20
  174.9 188.8 %all-gather.1 = bf16[8,1,128]{2,1,0:T(2,128)(2,1)S(1)} all-gather(bf16[1,1,128]{2,1,0:T(2,128)(2,1)S(1)} %bitcast.158), channel_id=1, replica_groups=mesh['rep'=4,'fsdp'=8] {'fsdp'}, dimensions={0}, use_global_device_ids=true | all-gather | bytes 2304 | tf_op jit(solution)/shard_map/all_gather | solution.py:159
  377.0 152.8 %collective-permute-done.2 = bf16[2304,1024]{1,0:T(8,128)(2,1)} collective-permute-done((bf16[2304,1024]{1,0:T(8,128)(2,1)}, bf16[2304,1024]{1,0:T(8,128)(2,1)}, u32[]{:S(2)}, u32[]{:S(2)}) %collective-permute-start.2) | collective-permute-done | bytes 4718624 | tf_op jit(solution)/shard_map/ppermute | solution.py:20
  529.9 5.1 constant_dynamic-update-slice_fusion.4
  538.8 5.0 constant_dynamic-update-slice_fusion
  543.8 2.7 fusion.53
  559.8 7.9 fusion.52
  567.7 8.9 multiply_convert_fusion.1
  576.7 12.1 %multiply_reduce_fusion = (bf16[1024]{0:T(1024)(128)(2,1)}, f32[128]{0:T(128)S(1)}, f32[128,1024]{1,0:T(8,128)S(1)}) fusion(f32[128,1024]{1,0:T(8,128)S(1)} %get-tuple-element.62, f32[128]{0:T(128)S(1)} %get-tuple-element.58, f32[1024]{0:T(1024)S(1)} %bitcast.144, bf16[1024,9216]{1,0:T(8,128)(2,1)} %all-gather.13.cloned.1.call-done, ...), kind=kOutput, calls=%fused_computation.46 | convolution fusion | flops 2421423104 | bytes 22289408 | tf_op jit(solution)/shard_map/dot_general | solution.py:133
  591.8 6.5 bitcast_convert_fusion
  598.3 5.7 fusion.2
  613.0 3.1 pad_maximum_fusion.3
  622.8 3.0 fusion.55
  634.2 33.2 %reduce-scatter.6.cloned.1.call-done = bf16[2,128,512]{2,1,0:T(8,128)(2,1)} async-done(((bf16[2,1024,512]{2,1,0:T(8,128)(2,1)}), bf16[2,128,512]{2,1,0:T(8,128)(2,1)}) %reduce-scatter.6.cloned.1.call-update) | async-done | bytes 262160 | tf_op jit(solution)/shard_map/reduce_scatter | solution.py:241
  677.2 4.4 convolution_convert_fusion.2
  681.8 6.6 convolution_convert_fusion.1
  689.0 10.9 convolution_convert_fusion
  700.0 4.0 reduce-scatter.10.cloned.1.call-done
  704.0 51.4 %reduce-scatter.8.cloned.1.call-done = bf16[128,2048]{1,0:T(8,128)(2,1)} async-done(((bf16[1024,2048]{1,0:T(8,128)(2,1)}), bf16[128,2048]{1,0:T(8,128)(2,1)}) %reduce-scatter.8.cloned.1.call-update) | async-done | bytes 524304 | tf_op jit(solution)/shard_map/reduce_scatter | solution.py:289
  755.5 100.2 %reduce-scatter.14.cloned.1.call-done = bf16[576,1024]{1,0:T(8,128)(2,1)} async-done(((bf16[4608,1024]{1,0:T(8,128)(2,1)}), bf16[576,1024]{1,0:T(8,128)(2,1)}) %reduce-scatter.14.cloned.1.call-update) | async-done | bytes 1179664 | tf_op jit(solution)/shard_map/reduce_scatter | solution.py:298
  855.7 188.8 %reduce-scatter.12.cloned.1.call-done = bf16[128,9216]{1,0:T(8,128)(2,1)} async-done(((bf16[1024,9216]{1,0:T(8,128)(2,1)}), bf16[128,9216]{1,0:T(8,128)(2,1)}) %reduce-scatter.12.cloned.1.call-update) | async-done | bytes 2359312 | tf_op jit(solution)/shard_map/reduce_scatter | solution.py:295
  1052.4 7.9 fusion.20
  1061.2 4.1 multiply_reduce_fusion.1
  1065.3 14.6 %all-reduce.6 = (bf16[1024]{0:T(1024)(128)(2,1)S(1)}, bf16[64]{0:T(256)(128)(2,1)S(1)}, bf16[64]{0:T(256)(128)(2,1)S(1)}, bf16[1024]{0:T(1024)(128)(2,1)S(1)}) all-reduce(bf16[1024]{0:T(1024)(128)(2,1)S(1)} %get-tuple-element.12, bf16[64]{0:T(256)(128)(2,1)S(1)} %fusion.25, ...), channel_id=7, replica_groups=mesh['rep'=4,'fsdp'=8] {'fsdp'}, use_global_device_ids=true, to_apply=%region_21.22.clone | all-reduce | flops 2176 | bytes 8704
  1080.2 10.5 all-reduce.8
  1093.8 58.6 %all-reduce.12.cloned.1.call-done = (bf16[128,2048]{1,0:T(8,128)(2,1)}, bf16[128,1024]{1,0:T(8,128)(2,1)}, bf16[128,9216]{1,0:T(8,128)(2,1)}, bf16[576,1024]{1,0:T(8,128)(2,1)}) async-done(((bf16[128,2048]{1,0:T(8,128)(2,1)}, bf16[128,1024]{1,0:T(8,128)(2,1)}, bf16[128,9216]{1,0:T(8,128)(2,1)}, bf16[576,1024]{1,0:T(8,128)(2,1)}), (bf16[128,2048]{1,0:T(8,128)(2,1)}, bf16[128,1024]{1,0:T(8,128)(2,1)}, ...) | async-done | bytes 4325392 | tf_op jit(solution)/shard_map/psum | solution.py:315
  1152.4 4.5 convert_element_type.164
  (250 shorter events, 98.3 us)
Async XLA Ops:
  7.2 52.3 %all-gather.7.cloned.1.call-start = ((), (), s32[]{:S(2)}) async-start(), calls=%async_computation.5 | async-start | bytes 4718592 | tf_op jit(solution)/shard_map/all_gather | solution.py:152
  7.9 535.9 %all-gather.9.cloned.1.call-start = ((), (), s32[]{:S(2)}) async-start(), calls=%async_computation.6 | async-start | bytes 2359296 | tf_op jit(solution)/shard_map/all_gather | solution.py:191
  40.3 19.2 %copy-start.52 = (bf16[64]{0:T(256)(128)(2,1)}, bf16[64]{0:T(256)(128)(2,1)S(1)}, u32[]{:S(2)}) copy-start(bf16[64]{0:T(256)(128)(2,1)S(1)} %get-tuple-element.18) | copy-start | bytes 388
  40.3 132.6 %copy-start.54 = (bf16[64]{0:T(256)(128)(2,1)}, bf16[64]{0:T(256)(128)(2,1)S(1)}, u32[]{:S(2)}) copy-start(bf16[64]{0:T(256)(128)(2,1)S(1)} %get-tuple-element.19) | copy-start | bytes 388
  40.3 24.4 %copy-start.49 = (f32[64]{0:T(128)}, f32[64]{0:T(128)S(1)}, u32[]{:S(2)}) copy-start(f32[64]{0:T(128)S(1)} %convert_element_type.142) | copy-start | bytes 772
  42.1 20.7 %copy-start.45 = (f32[128]{0:T(128)}, f32[128]{0:T(128)S(1)}, u32[]{:S(2)}) copy-start(f32[128]{0:T(128)S(1)} %get-tuple-element.56) | copy-start | bytes 1540
  42.2 22.5 %copy-start.32 = (f32[128,32]{0,1:T(8,128)}, f32[128,32]{0,1:T(8,128)S(1)}, u32[]{:S(2)}) copy-start(f32[128,32]{0,1:T(8,128)S(1)} %get-tuple-element.51) | copy-start | bytes 49156
  42.2 22.5 %copy-start.34 = (f32[128,32]{0,1:T(8,128)}, f32[128,32]{0,1:T(8,128)S(1)}, u32[]{:S(2)}) copy-start(f32[128,32]{0,1:T(8,128)S(1)} %get-tuple-element.52) | copy-start | bytes 49156
  63.7 35.5 %copy-start.14 = (f32[128,512]{1,0:T(8,128)}, f32[128,512]{1,0:T(8,128)S(1)}, u32[]{:S(2)}) copy-start(f32[128,512]{1,0:T(8,128)S(1)} %slice.71) | copy-start | bytes 786436
  63.9 35.4 %copy-start.12 = (f32[128,512]{0,1:T(8,128)}, f32[128,512]{0,1:T(8,128)S(1)}, u32[]{:S(2)}) copy-start(f32[128,512]{0,1:T(8,128)S(1)} %copy.97) | copy-start | bytes 786436
  66.1 491.0 %all-gather.11.cloned.1.call-start = ((), (), s32[]{:S(2)}) async-start(), calls=%async_computation.7 | async-start | bytes 2359296 | tf_op jit(solution)/shard_map/all_gather | solution.py:153
  66.8 493.0 %all-gather.13.cloned.1.call-start = ((), (), s32[]{:S(2)}) async-start(), calls=%async_computation.8 | async-start | bytes 21233664 | tf_op jit(solution)/shard_map/all_gather | solution.py:154
  67.4 600.0 %reduce-scatter.6.cloned.1.call-start = ((), (), s32[]{:S(2)}) async-start(), calls=%async_computation.9 | async-start | bytes 2359296 | tf_op jit(solution)/shard_map/reduce_scatter | solution.py:241
  67.4 31.8 %collective-permute-start = (bf16[576,1024]{1,0:T(8,128)(2,1)S(1)}, bf16[576,1024]{1,0:T(8,128)(2,1)S(1)}, u32[]{:S(2)}, u32[]{:S(2)}) collective-permute-start(bf16[576,1024]{1,0:T(8,128)(2,1)S(1)} %copy-done.2), channel_id=1, source_target_pairs={{0,7},{1,0},{2,1},{3,2},{4,3},{5,4},{6,5},{7,6},{8,15},{9,8},{10,9... | collective-permute-start | bytes 3538952 | tf_op jit(solution)/shard_map/ppermute | solution.py:20
  99.2 73.7 %copy-start.3 = (bf16[576,1024]{1,0:T(8,128)(2,1)}, bf16[576,1024]{1,0:T(8,128)(2,1)S(1)}, u32[]{:S(2)}) copy-start(bf16[576,1024]{1,0:T(8,128)(2,1)S(1)} %collective-permute-done) | copy-start | bytes 3538948
  99.4 75.5 %copy-start.51 = (bf16[128]{0:T(256)(128)(2,1)S(1)}, bf16[128]{0:T(256)(128)(2,1)}, u32[]{:S(2)}) copy-start(bf16[128]{0:T(256)(128)(2,1)} %param.21) | copy-start | bytes 772
  99.5 71.0 %collective-permute-start.1 = (bf16[1152,1024]{1,0:T(8,128)(2,1)S(1)}, bf16[1152,1024]{1,0:T(8,128)(2,1)S(1)}, u32[]{:S(2)}, u32[]{:S(2)}) collective-permute-start(bf16[1152,1024]{1,0:T(8,128)(2,1)S(1)} %pad_maximum_fusion.1), channel_id=1, source_target_pairs={{0,6},{1,7},{2,0},{3,1},{4,2},{5,3},{6,4},{7,5},{8,14},{9,15},{10,... | collective-permute-start | bytes 7077896 | tf_op jit(solution)/shard_map/ppermute | solution.py:20
  172.9 356.9 %collective-permute-start.2 = (bf16[2304,1024]{1,0:T(8,128)(2,1)}, bf16[2304,1024]{1,0:T(8,128)(2,1)}, u32[]{:S(2)}, u32[]{:S(2)}) collective-permute-start(bf16[2304,1024]{1,0:T(8,128)(2,1)} %pad_maximum_fusion), channel_id=1, source_target_pairs={{0,4},{1,5},{2,6},{3,7},{4,0},{5,1},{6,2},{7,3},{8,12},{9,13},{10,... | collective-permute-start | bytes 14155784 | tf_op jit(solution)/shard_map/ppermute | solution.py:20
  377.0 159.0 %copy-start.4 = (bf16[576,1024]{1,0:T(8,128)(2,1)S(1)}, bf16[576,1024]{1,0:T(8,128)(2,1)}, u32[]{:S(2)}) copy-start(bf16[576,1024]{1,0:T(8,128)(2,1)} %copy-done.3) | copy-start | bytes 3538948
  559.2 29.6 %copy-start.41 = (f32[128]{0:T(128)}, f32[128]{0:T(128)S(1)}, u32[]{:S(2)}) copy-start(f32[128]{0:T(128)S(1)} %get-tuple-element.58) | copy-start | bytes 1540
  576.7 12.1 %copy-start.23 = (bf16[128,4608]{1,0:T(8,128)(2,1)}, bf16[128,4608]{1,0:T(8,128)(2,1)S(1)}, u32[]{:S(2)}) copy-start(bf16[128,4608]{1,0:T(8,128)(2,1)S(1)} %get-tuple-element.29) | copy-start | bytes 3538948
  576.7 12.3 %copy-start.6 = (bf16[1024,1024]{1,0:T(8,128)(2,1)S(1)}, bf16[1024,1024]{1,0:T(8,128)(2,1)}, u32[]{:S(2)}) copy-start(bf16[1024,1024]{1,0:T(8,128)(2,1)} %all-gather.11.cloned.1.call-done) | copy-start | bytes 6291460
  616.1 88.0 %reduce-scatter.10.cloned.1.call-start = ((), (), s32[]{:S(2)}) async-start(), calls=%async_computation.11 | async-start | bytes 2359296 | tf_op jit(solution)/shard_map/reduce_scatter | solution.py:292
  618.2 137.3 %reduce-scatter.8.cloned.1.call-start = ((), (), s32[]{:S(2)}) async-start(), calls=%async_computation.10 | async-start | bytes 4718592 | tf_op jit(solution)/shard_map/reduce_scatter | solution.py:289
  625.9 46.1 %copy-start.13 = (f32[128,512]{0,1:T(8,128)S(1)}, f32[128,512]{0,1:T(8,128)}, u32[]{:S(2)}) copy-start(f32[128,512]{0,1:T(8,128)} %copy-done.12) | copy-start | bytes 786436
  681.7 174.0 %reduce-scatter.14.cloned.1.call-start = ((), (), s32[]{:S(2)}) async-start(), calls=%async_computation.13 | async-start | bytes 10616832 | tf_op jit(solution)/shard_map/reduce_scatter | solution.py:298
  688.4 356.0 %reduce-scatter.12.cloned.1.call-start = ((), (), s32[]{:S(2)}) async-start(), calls=%async_computation.12 | async-start | bytes 21233664 | tf_op jit(solution)/shard_map/reduce_scatter | solution.py:295
  699.9 345.8 %copy-start.39 = (f32[128,8]{0,1:T(8,128)S(1)}, f32[128,8]{0,1:T(8,128)}, u32[]{:S(2)}) copy-start(f32[128,8]{0,1:T(8,128)} %copy-done.37) | copy-start | bytes 12292
  699.9 346.0 %copy-start.15 = (f32[128,512]{1,0:T(8,128)S(1)}, f32[128,512]{1,0:T(8,128)}, u32[]{:S(2)}) copy-start(f32[128,512]{1,0:T(8,128)} %copy-done.14) | copy-start | bytes 786436
  699.9 347.0 %copy-start.11 = (f32[128,1024]{1,0:T(8,128)S(1)}, f32[128,1024]{1,0:T(8,128)}, u32[]{:S(2)}) copy-start(f32[128,1024]{1,0:T(8,128)} %slice.77) | copy-start | bytes 1572868
  699.9 452.4 %all-reduce.12.cloned.1.call-start = ((), (), s32[]{:S(2)}) async-start(), calls=%async_computation.14 | async-start | bytes 8650752 | tf_op jit(solution)/shard_map/psum | solution.py:315
  1060.3 32.5 %copy-start.50 = (f32[128]{0:T(128)S(1)}, f32[128]{0:T(128)}, u32[]{:S(2)}) copy-start(f32[128]{0:T(128)} %get-tuple-element.55) | copy-start | bytes 1540
  (37 other events, 185.5 us)
Sparse Core Ops, SparseCore 0:
  9.6 49.8 all-gather.6
  66.2 32.9 all-gather.8
  100.8 45.1 all-gather.10
  147.5 358.8 all-gather.12
  616.2 51.1 reduce-scatter.5
  669.6 34.4 reduce-scatter.9
  706.9 48.5 reduce-scatter.7
  757.8 97.8 reduce-scatter.13
  858.0 186.3 reduce-scatter.11
  1048.0 104.3 all-reduce.11
